TPU v7x, 128 devices: a whole 4x4x4 slice. The times are simulated.
128 devices in a mesh: dp: 32 (over z, x, y_lo), tensor: 4 (over y_hi, core).
Axes of the slice: x: 4, y: 4 (y_hi: 2, y_lo: 2; y = y_hi * 2 + y_lo), z: 4, core: 2. Of those that a mesh axis runs over, the one named last changes fastest.
Arguments:
- acts: bfloat16 [16384, 4096], P(('dp', 'tensor')), may hold values from -6 to 6
- out_grad: bfloat16 [16384, 16384], P('dp', 'tensor'), may hold values from -0.09375 to 0.09375
- projector: bfloat16 [4096, 512], replicated, may hold values from -0.09375 to 0.09375
- weight: bfloat16 [4096, 16384], P('dp', 'tensor'), may hold values from -6 to 6
- first_moment: float32 [4, 4096, 512], P('tensor', 'dp'), may hold values from -4 to 4
- second_moment: float32 [4, 4096, 512], P('tensor', 'dp'), may hold values from 0.01 to 1
Outputs:
- new_weight: bfloat16 [4096, 16384], P('dp', 'tensor')
- new_first: float32 [4, 4096, 512], P('tensor', 'dp')
- new_second: float32 [4, 4096, 512], P('tensor', 'dp')
All inputs are finite; a program needn't handle non-finite values.
Results may differ from a plain program's by a relative error of at most 0.015.
Values may be sent and summed in bfloat16 or wider, within the bound.
A program may use at most 128 MiB of HBM per device.

v0:
```python
import jax
import jax.numpy as jnp
from jax import lax
from jax.sharding import PartitionSpec as P

beta_first = 0.9
beta_second = 0.95
adam_step = 10
epsilon = 1e-08
step_rate = 0.5


def adam_moments(lowgrad, first_moment, second_moment):
    new_first = beta_first * first_moment + (1.0 - beta_first) * lowgrad
    new_second = beta_second * second_moment + (1.0 - beta_second) * lowgrad * lowgrad
    corrected_first = new_first / (1.0 - beta_first**adam_step)
    corrected_second = new_second / (1.0 - beta_second**adam_step)
    direction = (corrected_first / (jnp.sqrt(corrected_second) + epsilon)).astype(jnp.bfloat16)
    return (new_first, new_second, direction)


def per_device(acts, out_grad, projector, weight, first_moment, second_moment):
    whole_acts = lax.all_gather(acts, "tensor", axis=0, tiled=True)
    owned_grad = lax.psum_scatter(
        lax.dot_general(
            out_grad, whole_acts, (((0,), (0,)), ((), ())), preferred_element_type=jnp.float32
        ).astype(jnp.bfloat16),
        "dp",
        scatter_dimension=0,
        tiled=True,
    ).astype(jnp.float32)
    lowgrad = jnp.dot(
        owned_grad,
        projector.astype(jnp.float32),
        precision=lax.Precision.HIGHEST,
        preferred_element_type=jnp.float32,
    )
    new_first, new_second, direction = adam_moments(lowgrad, first_moment[0], second_moment[0])
    owned_update = lax.dot_general(
        projector, direction, (((1,), (1,)), ((), ())), preferred_element_type=jnp.float32
    ).astype(jnp.bfloat16)
    update = lax.all_to_all(owned_update, "dp", split_axis=0, concat_axis=1, tiled=True)
    new_weight = (weight.astype(jnp.float32) - step_rate * update.astype(jnp.float32)).astype(
        jnp.bfloat16
    )
    return (new_weight, new_first[None], new_second[None])


def solution(mesh):
    return jax.shard_map(
        per_device,
        mesh=mesh,
        in_specs=(
            P(("dp", "tensor"), None),
            P("dp", "tensor"),
            P(),
            P("dp", "tensor"),
            P("tensor", "dp", None),
            P("tensor", "dp", None),
        ),
        out_specs=(P("dp", "tensor"), P("tensor", "dp", None), P("tensor", "dp", None)),
        check_vma=False,
    )
```

profile of v0, /device:TPU:0, one launch (start us, length us, event | category | flops | bytes accessed | tf_op | source)
XLA Modules:
  0.0 826.6 jit_solution(7803383295628024617)
XLA Ops:
  7.2 0.0 all-gather.2.cloned.1.call-start
  7.2 0.7 all-gather.2.cloned.1.call-update
  7.9 0.0 reduce-scatter.2.cloned.1.call-start
  7.9 42.8 %all-gather.2.cloned.1.call-done = bf16[512,4096]{1,0:T(8,128)(2,1)} async-done(((bf16[128,4096]{1,0:T(8,128)(2,1)}), bf16[512,4096]{1,0:T(8,128)(2,1)}) %all-gather.2.cloned.1.call-update) | async-done | bytes 4194320 | tf_op jit(solution)/shard_map/all_gather | solution.py:23
  50.7 24.1 %convolution_convert_fusion = bf16[4096,4096]{1,0:T(8,128)(2,1)} fusion(bf16[512,4096]{1,0:T(8,128)(2,1)} %param.7, bf16[512,4096]{1,0:T(8,128)(2,1)} %all-gather.2.cloned.1.call-done), kind=kOutput, calls=%fused_computation | convolution fusion | flops 17196646400 | bytes 41943040 | tf_op jit(solution)/shard_map/dot_general | solution.py:25
  74.8 0.0 reduce-scatter.2.cloned.1.call-update
  74.9 0.0 copy-start.1
  74.9 0.0 copy-start.2
  74.9 708.0 %reduce-scatter.2.cloned.1.call-done = bf16[128,4096]{1,0:T(8,128)(2,1)} async-done(((bf16[4096,4096]{1,0:T(8,128)(2,1)}), bf16[128,4096]{1,0:T(8,128)(2,1)}) %reduce-scatter.2.cloned.1.call-update) | async-done | bytes 1048592 | tf_op jit(solution)/shard_map/reduce_scatter | solution.py:24
  782.9 0.0 copy-start
  782.9 3.4 fusion.15
  786.2 0.0 copy-done.1
  786.3 0.0 copy-done.2
  786.3 0.3 copy-done
  786.6 1.4 fusion
  788.1 1.3 copy.14
  789.3 7.3 all-to-all-start
  796.6 0.9 fusion.6
  797.5 17.2 %all-to-all-done = bf16[32,128,128]{1,2,0:T(8,128)(2,1)S(1)} async-done(((bf16[32,128,128]{1,2,0:T(8,128)(2,1)}), bf16[32,128,128]{1,2,0:T(8,128)(2,1)S(1)}, u32[]{:S(2)}, u32[]{:S(2)}) %all-to-all-start) | async-done | bytes 1048608 | tf_op jit(solution)/shard_map/all_to_all | solution.py:42
  814.7 0.2 convert_multiply_fusion
  814.9 1.9 copy.11
  816.8 3.0 subtract_convert_fusion
Async XLA Ops:
  7.2 43.5 %all-gather.2.cloned.1.call-start = ((), (), s32[]{:S(2)}) async-start(), calls=%async_computation.2 | async-start | bytes 5242880 | tf_op jit(solution)/shard_map/all_gather | solution.py:23
  7.9 775.0 %reduce-scatter.2.cloned.1.call-start = ((), (), s32[]{:S(2)}) async-start(), calls=%async_computation.3 | async-start | bytes 34603008 | tf_op jit(solution)/shard_map/reduce_scatter | solution.py:24
  74.9 711.4 %copy-start.1 = (f32[1,128,512]{2,1,0:T(8,128)S(1)}, f32[1,128,512]{2,1,0:T(8,128)}, u32[]{:S(2)}) copy-start(f32[1,128,512]{2,1,0:T(8,128)} %param.10) | copy-start | bytes 786436
  74.9 711.4 %copy-start.2 = (f32[1,128,512]{2,1,0:T(8,128)S(1)}, f32[1,128,512]{2,1,0:T(8,128)}, u32[]{:S(2)}) copy-start(f32[1,128,512]{2,1,0:T(8,128)} %param.11) | copy-start | bytes 786436
  782.9 3.7 copy-start
  789.3 25.3 %all-to-all-start = ((bf16[32,128,128]{1,2,0:T(8,128)(2,1)}), bf16[32,128,128]{1,2,0:T(8,128)(2,1)S(1)}, u32[]{:S(2)}, u32[]{:S(2)}) async-start(bf16[32,128,128]{1,2,0:T(8,128)(2,1)} %bitcast.31), calls=%async_computation.1 | async-start | bytes 2097152 | tf_op jit(solution)/shard_map/all_to_all | solution.py:42
Sparse Core Ops, SparseCore 0:
  9.7 40.9 all-gather.1
  75.0 707.8 reduce-scatter.1
where the time goes:
time: 827 us
  waiting for transfers between devices  769 us (93%)
  matrix products  29 us (4%)
  between operations  14.1 us (2%)
    reduce_scatter x1, waiting for transfers between devices, per_device(): lax.psum_scatter(lax.dot_general(out_grad, whole_acts, (((0,), (0,)), (()...  708 us
    all_gather x1, waiting for transfers between devices, per_device(): whole_acts = lax.all_gather(acts, 'tensor', axis=0, tiled=True)  42.8 us
    dot_general x1, matrix products, per_device(): lax.dot_general(out_grad, whole_acts, (((0,), (0,)), ((), ())), preferred...  24.1 us
    all_to_all x1, waiting for transfers between devices, per_device(): lax.all_to_all(owned_update, 'dp', split_axis=0, concat_axis=1, tiled=True)  17.2 us
  transfers between devices with their start and end apart: 3, of which 3 were waited for; matrix products, arithmetic and copies ran while one was open for 0% of the time, Pallas kernels for 0%

commit v1 on v0

--- a/solution.py
+++ b/solution.py
@@ -20,7 +20,9 @@
 
 
 def per_device(acts, out_grad, projector, weight, first_moment, second_moment):
-    whole_acts = lax.all_gather(acts, "tensor", axis=0, tiled=True)
+    last = jnp.stack([acts for _ in range(lax.axis_size("tensor"))])
+    arr_now = lax.all_to_all(last, "tensor", 0, 0)
+    whole_acts = jnp.concatenate(arr_now, axis=0)
     owned_grad = lax.psum_scatter(
         lax.dot_general(
             out_grad, whole_acts, (((0,), (0,)), ((), ())), preferred_element_type=jnp.float32

time: 827 us -> 837 us (1.012)
  blocking collectives: 0 us -> 54.3 us
  waiting for transfers between devices: 769 us -> 726 us
    all_to_all x0 -> x1, blocking collectives: none -> 54.3 us  [per_device(): arr_now = lax.all_to_all(last, 'tensor', 0, 0)]
    all_gather x1 -> x0, waiting for transfers between devices: 42.8 us -> none  [per_device(): whole_acts = lax.all_gather(acts, 'tensor', axis=0, tiled=True)]
  transfers between devices with their start and end apart: 3 -> 2, of which waited for: 3 -> 2; matrix products, arithmetic and copies ran while one was open for 0% -> 0% of each run, Pallas kernels for 0% -> 0%
where the time goes in v1:
time: 837 us
  waiting for transfers between devices  726 us (87%)
  blocking collectives  54.3 us (6%)
  matrix products  26.4 us (3%)
  between operations  14.1 us (2%)
    reduce_scatter x1, waiting for transfers between devices, per_device(): lax.psum_scatter(lax.dot_general(out_grad, whole_acts, (((0,), (0,)), (()...  708 us
    all_to_all x1, blocking collectives, per_device(): arr_now = lax.all_to_all(last, 'tensor', 0, 0)  54.3 us
    dot_general x1, matrix products, per_device(): lax.dot_general(out_grad, whole_acts, (((0,), (0,)), ((), ())), preferred...  21.6 us
    all_to_all x1, waiting for transfers between devices, per_device(): lax.all_to_all(owned_update, 'dp', split_axis=0, concat_axis=1, tiled=True)  17.2 us
  transfers between devices with their start and end apart: 2, of which 2 were waited for; matrix products, arithmetic and copies ran while one was open for 0% of the time, Pallas kernels for 0%

profile of v1, /device:TPU:0, one launch (start us, length us, event | category | flops | bytes accessed | tf_op | source)
XLA Modules:
  0.0 837.2 jit_solution(7284702812043701777)
XLA Ops:
  7.2 0.0 reduce-scatter.2.cloned.1.call-start
  7.2 1.7 stack.2
  8.9 0.0 copy-start.3
  8.9 54.3 %all_to_all.18 = bf16[4,128,4096]{2,1,0:T(8,128)(2,1)S(1)} all-to-all(bf16[4,128,4096]{2,1,0:T(8,128)(2,1)S(1)} %stack.2), channel_id=1, replica_groups=mesh['dp'=32,'tensor'=4] {'tensor'}, dimensions={0} | all-to-all | bytes 8388608 | tf_op jit(solution)/shard_map/all_to_all | solution.py:24
  63.2 0.0 copy-done.3
  63.2 21.6 %convolution_convert_fusion = bf16[4096,4096]{1,0:T(8,128)(2,1)} fusion(bf16[512,4096]{1,0:T(8,128)(2,1)S(1)} %copy-done.3, bf16[512,4096]{1,0:T(8,128)(2,1)S(1)} %bitcast.34), kind=kOutput, calls=%fused_computation | convolution fusion | flops 17196646400 | bytes 41943040 | tf_op jit(solution)/shard_map/dot_general | solution.py:27
  84.9 0.0 reduce-scatter.2.cloned.1.call-update
  84.9 0.0 copy-start.1
  84.9 0.0 copy-start.2
  84.9 708.5 %reduce-scatter.2.cloned.1.call-done = bf16[128,4096]{1,0:T(8,128)(2,1)} async-done(((bf16[4096,4096]{1,0:T(8,128)(2,1)}), bf16[128,4096]{1,0:T(8,128)(2,1)}) %reduce-scatter.2.cloned.1.call-update) | async-done | bytes 1048592 | tf_op jit(solution)/shard_map/reduce_scatter | solution.py:26
  793.4 0.0 copy-start
  793.4 3.4 fusion.15
  796.7 0.0 copy-done.1
  796.8 0.0 copy-done.2
  796.8 0.3 copy-done
  797.1 1.4 fusion
  798.6 1.3 copy.14
  799.8 7.3 all-to-all-start.1
  807.1 0.9 fusion.6
  808.0 17.2 %all-to-all-done.1 = bf16[32,128,128]{1,2,0:T(8,128)(2,1)S(1)} async-done(((bf16[32,128,128]{1,2,0:T(8,128)(2,1)}), bf16[32,128,128]{1,2,0:T(8,128)(2,1)S(1)}, u32[]{:S(2)}, u32[]{:S(2)}) %all-to-all-start.1) | async-done | bytes 1048608 | tf_op jit(solution)/shard_map/all_to_all | solution.py:44
  825.2 0.2 convert_multiply_fusion
  825.4 1.9 copy.11
  827.3 3.0 subtract_convert_fusion
Async XLA Ops:
  7.2 786.2 %reduce-scatter.2.cloned.1.call-start = ((), (), s32[]{:S(2)}) async-start(), calls=%async_computation.3 | async-start | bytes 34603008 | tf_op jit(solution)/shard_map/reduce_scatter | solution.py:26
  8.9 54.3 %copy-start.3 = (bf16[512,4096]{1,0:T(8,128)(2,1)S(1)}, bf16[512,4096]{1,0:T(8,128)(2,1)}, u32[]{:S(2)}) copy-start(bf16[512,4096]{1,0:T(8,128)(2,1)} %param.7) | copy-start | bytes 12582916
  84.9 711.9 %copy-start.1 = (f32[1,128,512]{2,1,0:T(8,128)S(1)}, f32[1,128,512]{2,1,0:T(8,128)}, u32[]{:S(2)}) copy-start(f32[1,128,512]{2,1,0:T(8,128)} %param.10) | copy-start | bytes 786436
  84.9 711.9 %copy-start.2 = (f32[1,128,512]{2,1,0:T(8,128)S(1)}, f32[1,128,512]{2,1,0:T(8,128)}, u32[]{:S(2)}) copy-start(f32[1,128,512]{2,1,0:T(8,128)} %param.11) | copy-start | bytes 786436
  793.4 3.7 copy-start
  799.8 25.4 %all-to-all-start.1 = ((bf16[32,128,128]{1,2,0:T(8,128)(2,1)}), bf16[32,128,128]{1,2,0:T(8,128)(2,1)S(1)}, u32[]{:S(2)}, u32[]{:S(2)}) async-start(bf16[32,128,128]{1,2,0:T(8,128)(2,1)} %bitcast.32), calls=%async_computation.2 | async-start | bytes 2097152 | tf_op jit(solution)/shard_map/all_to_all | solution.py:44
Sparse Core Ops, SparseCore 0:
  85.0 708.3 reduce-scatter.1
